TPU v7x, 32 devices: a whole 2x2x4 slice. The times are simulated.
32 devices in a mesh: req: 8 (over z, x), mlp: 4 (over y, core).
Axes of the slice: x: 2, y: 2, z: 4, core: 2. Of those that a mesh axis runs over, the one named last changes fastest.
Arguments:
- hidden_in: bfloat16 [256, 24, 2048], P('mlp', 'req'), may hold values from -6 to 6
- input_gain: float32 [2048], replicated, may hold values from 0.1 to 1.9
- query_weight: bfloat16 [2048, 2048], P(None, 'mlp'), may hold values from -0.125 to 0.125
- keyval_weight: bfloat16 [2048, 1024], P(None, 'mlp'), may hold values from -0.125 to 0.125
- query_gain: float32 [256], replicated, may hold values from 0.5 to 40
- key_gain: float32 [256], replicated, may hold values from 0.1 to 1.9
- out_weight: bfloat16 [2048, 2048], P('mlp'), may hold values from -0.125 to 0.125
- attn_gain: float32 [2048], replicated, may hold values from 0.1 to 1.9
- laurel_left: bfloat16 [2048, 64], replicated, may hold values from -0.125 to 0.125
- laurel_right: bfloat16 [64, 2048], replicated, may hold values from -0.75 to 0.75
- laurel_gain: float32 [2048], replicated, may hold values from 0.1 to 1.9
- ffn_gain: float32 [2048], replicated, may hold values from 0.1 to 1.9
- post_gain: float32 [2048], replicated, may hold values from 0.1 to 1.9
- gate_projection_matrix: bfloat16 [2048, 4096], P(None, 'mlp'), may hold values from -0.125 to 0.125
- up_projection_matrix: bfloat16 [2048, 4096], P(None, 'mlp'), may hold values from -0.125 to 0.125
- down_projection_matrix: bfloat16 [4096, 2048], P('mlp'), may hold values from -0.09375 to 0.09375
- page_pool: bfloat16 [16, 128, 1024], P('req'), may hold values from -6 to 6
- page_owner: int32 [2, 8], replicated, may hold values from 0 to 7, as said below
- page_slot: int32 [2, 8], replicated, may hold values from 0 to 1
- request_group: int32 [24], P('req'), may hold values from 0 to 1, as said below
- suffix_len: int32 [24], P('req'), may hold values from 64 to 256
Outputs:
- hidden_out: bfloat16 [256, 24, 2048], P('mlp', 'req')
- new_pages: bfloat16 [256, 24, 1024], P(None, 'req', 'mlp')
Inputs may be any that keep to these rules, and one draw needn't show every extreme that they name: `request_group`: each group has exactly 12 requests. The pairs (page_owner, page_slot) name every page of the pool exactly once.
All inputs are finite; a program needn't handle non-finite values.
Results may differ from a plain program's by a relative error of at most 0.013.
The roundings to bfloat16 on the way count: a program that leaves them out, or rounds other values in their place, can miss the bound.
Values may be sent and summed in bfloat16 or wider, within the bound.
No kernel may reach another device: no remote copies, remote signals or barrier semaphores. Data moves between devices by JAX's collectives and lax.ppermute only.
A program may use at most 128 MiB of HBM per device.

v0:
```python
import math
import jax
import jax.numpy as jnp
from jax import lax
from jax.sharding import PartitionSpec as P

PAGE = 128
PREFIX_PAGES = 8
EPS = 1e-06
INV_ROOT = 1.0 / math.sqrt(2.0)


def from_partner(value, axis, apart):
    return lax.ppermute(value, axis, [(i, i ^ 1 << apart) for i in range(lax.axis_size(axis))])


def rms_norm(values, norm_gain):
    values = values.astype(jnp.float32)
    return values * lax.rsqrt(jnp.mean(values * values, axis=-1, keepdims=True) + EPS) * norm_gain


def rotary(values, first_row):
    row_count = values.shape[0]
    halfway = values.shape[-1] // 2
    frequency = 1000000.0 ** (-jnp.arange(halfway, dtype=jnp.float32) / halfway)
    positions = (first_row + jnp.arange(row_count)).astype(jnp.float32)
    angles = positions[:, None] * frequency[None, :]
    cos_table = jnp.cos(angles)[:, None, None, :]
    sin_table = jnp.sin(angles)[:, None, None, :]
    first_half = values[..., :halfway]
    second_half = values[..., halfway:]
    return jnp.concatenate(
        [
            first_half * cos_table - second_half * sin_table,
            second_half * cos_table + first_half * sin_table,
        ],
        axis=-1,
    )


def local(
    hidden_in,
    input_gain,
    query_weight,
    keyval_weight,
    query_gain,
    key_gain,
    out_weight,
    attn_gain,
    laurel_left,
    laurel_right,
    laurel_gain,
    ffn_gain,
    post_gain,
    gate_projection_matrix,
    up_projection_matrix,
    down_projection_matrix,
    page_pool,
    page_owner,
    page_slot,
    request_group,
    suffix_len,
):
    mlp_index = lax.axis_index("mlp")
    part_rows = hidden_in.shape[0]
    local_reqs = hidden_in.shape[1]
    head_size = query_gain.shape[0]
    prefix_len = PREFIX_PAGES * PAGE
    parity = mlp_index % 2
    kv_head = mlp_index // 2
    query_cols = query_weight.shape[1]
    heads_here = query_cols // head_size
    active_rows = rms_norm(hidden_in, input_gain).astype(jnp.bfloat16)
    active_part = lax.all_gather(active_rows, "mlp", axis=0, tiled=True)
    first_row = jnp.int32(0)
    row_count = active_part.shape[0]
    project_queries = jnp.einsum(
        "trd,dc->trc", active_part, query_weight, preferred_element_type=jnp.float32
    )
    project_queries = project_queries.reshape(row_count, local_reqs, heads_here, head_size)
    project_queries = rotary(rms_norm(project_queries, query_gain), prefix_len + first_row)
    quarter = jnp.einsum(
        "trd,dc->trc", active_part, keyval_weight, preferred_element_type=jnp.float32
    )
    quarter = quarter.reshape(row_count, local_reqs, 1, head_size)
    as_keys = rotary(rms_norm(quarter, key_gain), prefix_len + first_row)
    as_values = rms_norm(quarter, 1.0)
    quarter = jnp.where(parity == 0, as_keys, as_values)
    joined = jnp.concatenate(
        [
            project_queries.reshape(row_count, local_reqs, query_cols),
            quarter.reshape(row_count, local_reqs, head_size),
        ],
        axis=-1,
    )
    projected = joined.astype(jnp.bfloat16)
    full_rows = projected.shape[0]
    queries = projected[..., :query_cols]
    quarter = projected[..., query_cols:]
    partner = from_partner(quarter, "mlp", 0)
    all_keys = jnp.where(parity == 0, quarter, partner)
    all_values = jnp.where(parity == 0, partner, quarter)
    live_full = jnp.arange(full_rows)[:, None] < suffix_len[None, :]
    new_pages = jnp.where(live_full[:, :, None], quarter, jnp.zeros_like(quarter))
    own_pages = lax.dynamic_slice_in_dim(page_pool, kv_head * 2 * head_size, 2 * head_size, 2)
    pool_pages = page_pool.shape[0]
    whole_pool = lax.all_gather(own_pages, "req", axis=0, tiled=True)
    page_ids = page_owner * pool_pages + page_slot
    group_count = page_ids.shape[0]
    selector = (request_group[:, None] == jnp.arange(group_count, dtype=jnp.int32)[None, :]).astype(
        jnp.int32
    )
    wanted = jnp.dot(selector, page_ids)
    prefix_kv = jnp.take(whole_pool, wanted.reshape(-1), axis=0).reshape(
        local_reqs, prefix_len, 2 * head_size
    )
    causal = jnp.arange(full_rows)[None, :] <= jnp.arange(full_rows)[:, None]
    score_scale = head_size ** (-0.5)

    def attend(req_index):
        query_rows = lax.dynamic_index_in_dim(queries, req_index, 1, keepdims=False).reshape(
            full_rows, heads_here, head_size
        )
        prefix_rows = lax.dynamic_index_in_dim(prefix_kv, req_index, 0, keepdims=False)
        keys_here = jnp.concatenate(
            [
                prefix_rows[:, :head_size],
                lax.dynamic_index_in_dim(all_keys, req_index, 1, keepdims=False),
            ],
            axis=0,
        )
        values_here = jnp.concatenate(
            [
                prefix_rows[:, head_size:],
                lax.dynamic_index_in_dim(all_values, req_index, 1, keepdims=False),
            ],
            axis=0,
        )
        live_count = lax.dynamic_index_in_dim(suffix_len, req_index, 0, keepdims=False)
        suffix_ok = causal & (jnp.arange(full_rows)[None, :] < live_count)
        allowed = jnp.concatenate(
            [jnp.ones((full_rows, prefix_len), dtype=bool), suffix_ok], axis=1
        )
        scores = (
            jnp.einsum("thd,sd->hts", query_rows, keys_here, preferred_element_type=jnp.float32)
            * score_scale
        )
        scores = jnp.where(allowed[None], scores, -jnp.inf)
        row_peak = jnp.max(scores, axis=-1, keepdims=True)
        exp_terms = jnp.exp(scores - row_peak)
        totals = jnp.sum(exp_terms, axis=-1)
        weights = exp_terms.astype(jnp.bfloat16)
        mixed_rows = jnp.einsum(
            "hts,sd->thd", weights, values_here, preferred_element_type=jnp.float32
        )
        mixed_rows = mixed_rows / jnp.transpose(totals)[:, :, None]
        return mixed_rows.reshape(full_rows, query_cols).astype(jnp.bfloat16)

    attended = lax.map(attend, jnp.arange(local_reqs))
    local_row_block = attended
    attn_summed = lax.psum_scatter(
        jnp.einsum(
            "rtc,cd->trd", local_row_block, out_weight, preferred_element_type=jnp.float32
        ).astype(jnp.bfloat16),
        "mlp",
        scatter_dimension=0,
        tiled=True,
    ).astype(jnp.float32)
    laurel_mid = jnp.einsum(
        "trd,dk->trk", active_rows, laurel_left, preferred_element_type=jnp.float32
    ).astype(jnp.bfloat16)
    laurel_out = active_rows.astype(jnp.float32) + rms_norm(
        jnp.einsum("trk,kd->trd", laurel_mid, laurel_right, preferred_element_type=jnp.float32),
        laurel_gain,
    )
    residual = (
        hidden_in.astype(jnp.float32) + rms_norm(attn_summed, attn_gain) + laurel_out
    ) * INV_ROOT
    ffn_in = rms_norm(residual, ffn_gain).astype(jnp.bfloat16)
    incoming_rows = lax.all_gather(ffn_in, "mlp", axis=0, tiled=True)
    gate_portion = jnp.einsum(
        "ghc,cu->ghu", incoming_rows, gate_projection_matrix, preferred_element_type=jnp.float32
    )
    up_portion = jnp.einsum(
        "ghc,cu->ghu", incoming_rows, up_projection_matrix, preferred_element_type=jnp.float32
    )
    expanded = (jax.nn.gelu(gate_portion, approximate=True) * up_portion).astype(jnp.bfloat16)
    local_row_block = expanded
    ffn_summed = lax.psum_scatter(
        jnp.einsum(
            "wjk,kx->wjx",
            local_row_block,
            down_projection_matrix,
            preferred_element_type=jnp.float32,
        ).astype(jnp.bfloat16),
        "mlp",
        scatter_dimension=0,
        tiled=True,
    ).astype(jnp.float32)
    own_positions = mlp_index * part_rows + jnp.arange(part_rows)
    live_part = own_positions[:, None] < suffix_len[None, :]
    output = residual + rms_norm(ffn_summed, post_gain)
    hidden_out = jnp.where(live_part[:, :, None], output, 0.0).astype(jnp.bfloat16)
    return (hidden_out, new_pages)


def solution(mesh):
    placed = (
        P("mlp", "req", None),
        P(),
        P(None, "mlp"),
        P(None, "mlp"),
        P(),
        P(),
        P("mlp", None),
        P(),
        P(),
        P(),
        P(),
        P(),
        P(),
        P(None, "mlp"),
        P(None, "mlp"),
        P("mlp", None),
        P("req", None, None),
        P(),
        P(),
        P("req"),
        P("req"),
    )
    return jax.shard_map(
        local,
        mesh=mesh,
        in_specs=placed,
        out_specs=(P("mlp", "req", None), P(None, "req", "mlp")),
        check_vma=False,
    )
```

profile of v0, /device:TPU:0, one launch (start us, length us, event | category | flops | bytes accessed | tf_op | source)
XLA Modules:
  0.0 296.1 jit_solution(11078036066806763758)
XLA Ops:
  7.3 1.8 constant_dynamic-slice_fusion.3
  9.2 1.4 fusion.56
  10.6 1.8 fusion.58
  14.2 48.7 %all-gather.4.cloned.1.call-done = bf16[16,128,512]{2,1,0:T(8,128)(2,1)} async-done(((bf16[2,128,512]{2,1,0:T(8,128)(2,1)}), bf16[16,128,512]{2,1,0:T(8,128)(2,1)}) %all-gather.4.cloned.1.call-update) | async-done | bytes 2097168 | tf_op jit(solution)/shard_map/all_gather | solution.py:107
  62.9 4.1 %gather_fusion = bf16[24,128,512]{2,1,0:T(8,128)(2,1)} fusion(bf16[16,128,512]{2,1,0:T(8,128)(2,1)} %all-gather.4.cloned.1.call-done, s32[1024]{0:T(1024)S(1)} %pad_clamp_fusion), kind=kCustom, calls=%fused_computation | custom fusion | bytes 6291552 | tf_op jit(solution)/shard_map/jit(_take)/gather | solution.py:114
  67.0 3.4 %bitcast_select_fusion = bf16[3,1024,512]{2,1,0:T(8,128)(2,1)} fusion(pred[3,1024]{1,0:T(4,128)(4,1)S(1)} %bitcast.122, bf16[3,1024,512]{2,1,0:T(8,128)(2,1)} %bitcast.115), kind=kLoop, calls=%fused_computation.47 | loop fusion | flops 1572864 | bytes 6294528 | tf_op jit(solution)/shard_map/jit(_take)/select_n | solution.py:114
  70.4 21.1 %all-gather.6.cloned.1.call-done = bf16[256,3,2048]{2,0,1:T(8,128)(2,1)} async-done(((bf16[64,3,2048]{2,0,1:T(8,128)(2,1)}), bf16[256,3,2048]{2,0,1:T(8,128)(2,1)}) %all-gather.6.cloned.1.call-update) | async-done | bytes 3145744 | tf_op jit(solution)/shard_map/all_gather | solution.py:74
  91.5 5.5 %fusion.45 = f32[256,3,512]{2,0,1:T(8,128)} fusion(bf16[256,3,2048]{2,0,1:T(8,128)(2,1)} %all-gather.6.cloned.1.call-done, bf16[2048,512]{1,0:T(8,128)(2,1)} %param.25), kind=kOutput, calls=%fused_computation.53 | convolution fusion | flops 1610612736 | bytes 6815744 | tf_op jit(solution)/shard_map/trd,dc->trc/dot_general | solution.py:77
  97.0 3.1 %reshape.241 = f32[256,3,2,256]{3,2,0,1:T(2,128)} reshape(f32[256,3,512]{2,0,1:T(8,128)} %fusion.45) | data formatting | bytes 3145728 | tf_op jit(solution)/shard_map/reshape | solution.py:80
  100.1 2.3 multiply_reduce_fusion.2
  102.4 3.6 %copy.57 = f32[256,3,2,256]{0,3,2,1:T(8,128)} copy(f32[256,3,2,256]{3,2,0,1:T(2,128)} %reshape.241) | data formatting | bytes 3145728 | tf_op jit(solution)/shard_map/reshape | solution.py:80
  106.1 4.2 %multiply_reduce_fusion.3 = (f32[256,3]{0,1:T(4,128)S(1)}, f32[256,3,256]{0,2,1:T(8,128)}) fusion(bf16[256,3,2048]{2,0,1:T(8,128)(2,1)} %all-gather.6.cloned.1.call-done, bf16[2048,256]{1,0:T(8,128)(2,1)} %param.26), kind=kOutput, calls=%fused_computation.85 | convolution fusion | flops 805698816 | bytes 4983808 | tf_op jit(solution)/shard_map/trd,dc->trc/dot_general | solution.py:82
  110.4 1.3 multiply_bitcast_fusion
  111.9 1.6 broadcast_select_fusion
  114.3 1.0 pad_maximum_fusion
  115.3 0.9 broadcast_select_fusion.1
  116.2 32.3 %while.11 = (s32[]{:T(128)}, bf16[3,256,512]{1,2,0:T(8,128)(2,1)}, s32[3]{0:T(128)S(1)}, bf16[3,1024,512]{2,1,0:T(8,128)(2,1)}, bf16[256,3,256]{0,2,1:T(8,128)(2...) while((s32[]{:T(128)}, bf16[3,256,512]{1,2,0:T(8,128)(2,1)}, ...), condition=%wide.region_6.7_spmd.clone, body=%wide.region_3.6_spmd.clone.sunk | while | flops 678690048 | bytes 18361092 | solution.py:159
  119.8 1.7 constant_dynamic-slice_fusion.6
  121.5 1.0 constant_dynamic-slice_fusion.7
  122.5 0.7 copy.76
  123.3 1.3 dynamic-slice_bitcast_fusion.2
  126.2 0.7 constant_dynamic-update-slice_fusion.2
  130.6 1.7 constant_dynamic-slice_fusion.6
  132.3 1.0 constant_dynamic-slice_fusion.7
  133.2 0.7 copy.76
  134.1 1.3 dynamic-slice_bitcast_fusion.2
  137.0 0.7 constant_dynamic-update-slice_fusion.2
  141.3 1.7 constant_dynamic-slice_fusion.6
  143.0 1.0 constant_dynamic-slice_fusion.7
  144.0 0.7 copy.76
  144.9 1.3 dynamic-slice_bitcast_fusion.2
  147.8 0.7 constant_dynamic-update-slice_fusion.2
  148.5 4.6 %fusion.43 = bf16[256,3,2048]{2,0,1:T(8,128)(2,1)} fusion(bf16[3,256,512]{1,2,0:T(8,128)(2,1)} %get-tuple-element.49, bf16[512,2048]{1,0:T(8,128)(2,1)S(1)} %copy-done), kind=kOutput, calls=%fused_computation.48 | convolution fusion | flops 1612185600 | bytes 6029312 | tf_op jit(solution)/shard_map/rtc,cd->trd/dot_general | solution.py:162
  153.4 0.7 copy-done.8
  154.1 2.2 multiply_reduce_fusion.1
  156.4 34.8 %reduce-scatter.3.cloned.1.call-done = bf16[64,3,2048]{2,0,1:T(8,128)(2,1)} async-done(((bf16[256,3,2048]{2,0,1:T(8,128)(2,1)}), bf16[64,3,2048]{2,0,1:T(8,128)(2,1)}) %reduce-scatter.3.cloned.1.call-update) | async-done | bytes 786448 | tf_op jit(solution)/shard_map/reduce_scatter | solution.py:161
  191.2 1.4 fusion.49
  192.6 2.5 multiply_reduce_fusion
  195.1 1.1 copy-done.1
  196.3 1.1 multiply_convert_fusion
  197.4 28.6 %all-gather.8.cloned.1.call-done = bf16[256,3,2048]{2,0,1:T(8,128)(2,1)} async-done(((bf16[64,3,2048]{2,0,1:T(8,128)(2,1)}), bf16[256,3,2048]{2,0,1:T(8,128)(2,1)}) %all-gather.8.cloned.1.call-update) | async-done | bytes 3145744 | tf_op jit(solution)/shard_map/all_gather | solution.py:180
  226.1 8.3 %fusion.29 = f32[256,3,1024]{2,0,1:T(8,128)} fusion(bf16[256,3,2048]{2,0,1:T(8,128)(2,1)} %all-gather.8.cloned.1.call-done, bf16[2048,1024]{1,0:T(8,128)(2,1)} %param.36), kind=kOutput, calls=%fused_computation.34 | convolution fusion | flops 3221225472 | bytes 10485760 | tf_op jit(solution)/shard_map/ghc,cu->ghu/dot_general | solution.py:181
  234.3 12.8 %fusion.31 = bf16[256,3,2048]{2,0,1:T(8,128)(2,1)} fusion(bf16[1024,2048]{1,0:T(8,128)(2,1)} %param.38, f32[256,3,1024]{2,0,1:T(8,128)} %fusion.29, bf16[256,3,2048]{2,0,1:T(8,128)(2,1)} %all-gather.8.cloned.1.call-done, bf16[2048,1024]{1,0:T(8,128)(2,1)} %param.37), kind=kOutput, calls=%fused_computation.37 | convolution fusion | flops 6451888128 | bytes 17825792 | tf_op jit(solution)/shard_map/wjk,kx->wjx/dot_general | solution.py:190
  247.2 0.9 copy-done.7
  248.1 0.9 copy.61
  249.0 36.2 %reduce-scatter.5.cloned.1.call-done = bf16[64,3,2048]{2,0,1:T(8,128)(2,1)} async-done(((bf16[256,3,2048]{2,0,1:T(8,128)(2,1)}), bf16[64,3,2048]{2,0,1:T(8,128)(2,1)}) %reduce-scatter.5.cloned.1.call-update) | async-done | bytes 786448 | tf_op jit(solution)/shard_map/reduce_scatter | solution.py:189
  285.2 1.4 fusion.51
  286.6 2.9 fusion.55
  (114 shorter events, 13.9 us)
Async XLA Ops:
  7.2 141.3 %copy-start = (bf16[512,2048]{1,0:T(8,128)(2,1)S(1)}, bf16[512,2048]{1,0:T(8,128)(2,1)}, u32[]{:S(2)}) copy-start(bf16[512,2048]{1,0:T(8,128)(2,1)} %param.29) | copy-start | bytes 6291460
  7.2 3.4 %copy-start.2 = (bf16[64,3,2048]{2,0,1:T(8,128)(2,1)S(1)}, bf16[64,3,2048]{2,0,1:T(8,128)(2,1)}, u32[]{:S(2)}) copy-start(bf16[64,3,2048]{2,0,1:T(8,128)(2,1)} %param.23) | copy-start | bytes 2359300
  7.2 5.3 %copy-start.18 = (s32[3]{0:T(128)S(1)}, s32[3]{0:T(128)}, u32[]{:S(2)}) copy-start(s32[3]{0:T(128)} %param.42) | copy-start | bytes 40
  7.2 5.3 %copy-start.16 = (s32[2,8]{1,0:T(2,128)S(1)}, s32[2,8]{1,0:T(2,128)}, u32[]{:S(2)}) copy-start(s32[2,8]{1,0:T(2,128)} %param.41) | copy-start | bytes 196
  7.2 5.3 %copy-start.17 = (s32[2,8]{1,0:T(2,128)S(1)}, s32[2,8]{1,0:T(2,128)}, u32[]{:S(2)}) copy-start(s32[2,8]{1,0:T(2,128)} %param.40) | copy-start | bytes 196
  7.2 5.8 %copy-start.19 = (s32[3]{0:T(128)S(1)}, s32[3]{0:T(128)}, u32[]{:S(2)}) copy-start(s32[3]{0:T(128)} %param.43) | copy-start | bytes 40
  7.2 55.7 %all-gather.4.cloned.1.call-start = ((), (), s32[]{:S(2)}) async-start(), calls=%async_computation.2 | async-start | bytes 2359296 | tf_op jit(solution)/shard_map/all_gather | solution.py:107
  9.1 82.4 %all-gather.6.cloned.1.call-start = ((), (), s32[]{:S(2)}) async-start(), calls=%async_computation.3 | async-start | bytes 3932160 | tf_op jit(solution)/shard_map/all_gather | solution.py:74
  12.4 178.8 %reduce-scatter.3.cloned.1.call-start = ((), (), s32[]{:S(2)}) async-start(), calls=%async_computation.4 | async-start | bytes 3932160 | tf_op jit(solution)/shard_map/reduce_scatter | solution.py:161
  110.4 1.5 copy-start.6
  111.7 2.0 copy-start.4
  111.8 2.0 copy-start.15
  113.5 1.7 collective-permute-start
  114.3 2.0 copy-start.20
  123.3 1.4 copy-start.3
  123.3 1.4 copy-start.5
  134.1 1.4 copy-start.3
  134.1 1.4 copy-start.5
  144.9 1.4 copy-start.3
  144.9 1.4 copy-start.5
  153.1 0.9 copy-start.8
  153.1 1.0 copy-start.9
  153.1 1.0 copy-start.10
  153.1 39.5 %copy-start.11 = (f32[2048]{0:T(1024)S(1)}, f32[2048]{0:T(1024)}, u32[]{:S(2)}) copy-start(f32[2048]{0:T(1024)} %param.33) | copy-start | bytes 24580
  153.2 39.5 %copy-start.12 = (f32[2048]{0:T(1024)S(1)}, f32[2048]{0:T(1024)}, u32[]{:S(2)}) copy-start(f32[2048]{0:T(1024)} %param.30) | copy-start | bytes 24580
  153.2 72.9 %all-gather.8.cloned.1.call-start = ((), (), s32[]{:S(2)}) async-start(), calls=%async_computation.5 | async-start | bytes 3932160 | tf_op jit(solution)/shard_map/all_gather | solution.py:180
  192.6 3.6 %copy-start.13 = (f32[2048]{0:T(1024)S(1)}, f32[2048]{0:T(1024)}, u32[]{:S(2)}) copy-start(f32[2048]{0:T(1024)} %param.34) | copy-start | bytes 24580
  195.1 1.1 copy-start.1
  197.4 87.9 %reduce-scatter.5.cloned.1.call-start = ((), (), s32[]{:S(2)}) async-start(), calls=%async_computation.6 | async-start | bytes 3932160 | tf_op jit(solution)/shard_map/reduce_scatter | solution.py:189
  247.1 1.0 copy-start.7
  247.1 39.5 %copy-start.14 = (f32[2048]{0:T(1024)S(1)}, f32[2048]{0:T(1024)}, u32[]{:S(2)}) copy-start(f32[2048]{0:T(1024)} %param.35) | copy-start | bytes 24580
Sparse Core Ops, SparseCore 0:
  10.8 52.0 all-gather.3
  64.5 27.0 all-gather.5
  153.3 37.9 reduce-scatter.2
  197.5 28.5 all-gather.7
  247.2 37.9 reduce-scatter.4
where the time goes:
time: 297 us; the launch traced here: 296 us
  waiting for transfers between devices  170 us (57%)
  matrix products  40.9 us (14%)
  local copies, waits for them, and re-layouts  37.5 us (13%)
  other arithmetic  28 us (9%)
  between operations  14.1 us (5%)
  loops' own time  5.32 us (2%)
    all_gather x1, waiting for transfers between devices, local(): whole_pool = lax.all_gather(own_pages, 'req', axis=0, tiled=True)  48.7 us
    reduce_scatter x1, waiting for transfers between devices, local(): lax.psum_scatter(jnp.einsum('wjk,kx->wjx', local_row_block, down_projecti...  36.2 us
    reduce_scatter x1, waiting for transfers between devices, local(): lax.psum_scatter(jnp.einsum('rtc,cd->trd', local_row_block, out_weight, p...  34.8 us
    all_gather x1, waiting for transfers between devices, local(): incoming_rows = lax.all_gather(ffn_in, 'mlp', axis=0, tiled=True)  28.6 us
    all_gather x1, waiting for transfers between devices, local(): active_part = lax.all_gather(active_rows, 'mlp', axis=0, tiled=True)  21.1 us
    dot_general x1, matrix products, local(): jnp.einsum('wjk,kx->wjx', local_row_block, down_projection_matrix, prefer...  12.8 us
    reduce_sum x5, other arithmetic, rms_norm(): jnp.mean(values * values, axis=-1, keepdims=True) + EPS  8.93 us
    dot_general x1, matrix products, local(): jnp.einsum('ghc,cu->ghu', incoming_rows, gate_projection_matrix, preferre...  8.26 us
  transfers between devices with their start and end apart: 6, of which 5 were waited for; matrix products, arithmetic and copies ran while one was open for 6% of the time, Pallas kernels for 0%

commit v1 on v0

--- a/solution.py
+++ b/solution.py
@@ -177,7 +177,12 @@
         hidden_in.astype(jnp.float32) + rms_norm(attn_summed, attn_gain) + laurel_out
     ) * INV_ROOT
     ffn_in = rms_norm(residual, ffn_gain).astype(jnp.bfloat16)
-    incoming_rows = lax.all_gather(ffn_in, "mlp", axis=0, tiled=True)
+    ring = [ffn_in]
+    for hop in range(3):
+        ring.append(lax.ppermute(ring[-1], "mlp", [(dev, (dev + 1) % 4) for dev in range(4)]))
+    incoming_rows = jnp.roll(
+        jnp.concatenate(ring[::-1], axis=0), (lax.axis_index("mlp") + 1) * ring[0].shape[0], axis=0
+    )
     gate_portion = jnp.einsum(
         "ghc,cu->ghu", incoming_rows, gate_projection_matrix, preferred_element_type=jnp.float32
     )

time: 297 us -> 321 us (1.081)
  local copies, waits for them, and re-layouts: 37.5 us -> 51.9 us
  waiting for transfers between devices: 170 us -> 176 us
    ppermute x0 -> x3, waiting for transfers between devices: none -> 34.6 us  [local(): lax.ppermute(ring[-1], 'mlp', [(dev, (dev + 1) % 4) for dev in range(4)])]
    all_gather x1 -> x0, waiting for transfers between devices: 28.6 us -> none  [local(): incoming_rows = lax.all_gather(ffn_in, 'mlp', axis=0, tiled=True)]
    unnamed x41 -> x53, local copies, waits for them, and re-layouts: 3.84 us -> 10.8 us
    dot_general x3, matrix products: 1.67 us -> 7.12 us  [attend(): jnp.einsum('hts,sd->thd', weights, values_here, preferred_element_type=jn...]
    while x12, local copies, waits for them, and re-layouts: 0.03 us -> 4.57 us
  transfers between devices with their start and end apart: 6 -> 8, of which waited for: 5 -> 7; matrix products, arithmetic and copies ran while one was open for 6% -> 6% of each run, Pallas kernels for 0% -> 0%
where the time goes in v1:
time: 321 us; the launch traced here: 320 us
  waiting for transfers between devices  176 us (55%)
  local copies, waits for them, and re-layouts  51.9 us (16%)
  matrix products  42.3 us (13%)
  other arithmetic  29.1 us (9%)
  between operations  14.2 us (4%)
  loops' own time  5.93 us (2%)
    all_gather x1, waiting for transfers between devices, local(): whole_pool = lax.all_gather(own_pages, 'req', axis=0, tiled=True)  48.8 us
    reduce_scatter x1, waiting for transfers between devices, local(): lax.psum_scatter(jnp.einsum('wjk,kx->wjx', local_row_block, down_projecti...  36.2 us
    reduce_scatter x1, waiting for transfers between devices, local(): lax.psum_scatter(jnp.einsum('rtc,cd->trd', local_row_block, out_weight, p...  34.9 us
    ppermute x3, waiting for transfers between devices, local(): lax.ppermute(ring[-1], 'mlp', [(dev, (dev + 1) % 4) for dev in range(4)])  34.6 us
    all_gather x1, waiting for transfers between devices, local(): active_part = lax.all_gather(active_rows, 'mlp', axis=0, tiled=True)  21.1 us
    dot_general x1, matrix products, local(): jnp.einsum('wjk,kx->wjx', local_row_block, down_projection_matrix, prefer...  12.8 us
    unnamed x53, local copies, waits for them, and re-layouts  10.8 us
    reduce_sum x5, other arithmetic, rms_norm(): jnp.mean(values * values, axis=-1, keepdims=True) + EPS  8.94 us
  transfers between devices with their start and end apart: 8, of which 7 were waited for; matrix products, arithmetic and copies ran while one was open for 6% of the time, Pallas kernels for 0%

profile of v1, /device:TPU:0, one launch (start us, length us, event | category | flops | bytes accessed | tf_op | source)
XLA Modules:
  0.0 319.7 jit_solution(2733658269831197614)
XLA Ops:
  7.3 1.8 constant_dynamic-slice_fusion.3
  9.2 1.4 fusion.60
  10.6 1.8 fusion.62
  14.1 48.8 %all-gather.3.cloned.1.call-done = bf16[16,128,512]{2,1,0:T(8,128)(2,1)} async-done(((bf16[2,128,512]{2,1,0:T(8,128)(2,1)}), bf16[16,128,512]{2,1,0:T(8,128)(2,1)}) %all-gather.3.cloned.1.call-update) | async-done | bytes 2097168 | tf_op jit(solution)/shard_map/all_gather | solution.py:107
  62.9 4.2 %gather_fusion = bf16[24,128,512]{2,1,0:T(8,128)(2,1)} fusion(bf16[16,128,512]{2,1,0:T(8,128)(2,1)} %all-gather.3.cloned.1.call-done, s32[1024]{0:T(1024)S(1)} %pad_clamp_fusion), kind=kCustom, calls=%fused_computation | custom fusion | bytes 6291552 | tf_op jit(solution)/shard_map/jit(_take)/gather | solution.py:114
  67.0 3.4 %bitcast_select_fusion = bf16[3,1024,512]{2,1,0:T(8,128)(2,1)} fusion(pred[3,1024]{1,0:T(4,128)(4,1)S(1)} %bitcast.120, bf16[3,1024,512]{2,1,0:T(8,128)(2,1)} %bitcast.113), kind=kLoop, calls=%fused_computation.47 | loop fusion | flops 1572864 | bytes 6294528 | tf_op jit(solution)/shard_map/jit(_take)/select_n | solution.py:114
  70.4 21.1 %all-gather.5.cloned.1.call-done = bf16[256,3,2048]{2,0,1:T(8,128)(2,1)} async-done(((bf16[64,3,2048]{2,0,1:T(8,128)(2,1)}), bf16[256,3,2048]{2,0,1:T(8,128)(2,1)}) %all-gather.5.cloned.1.call-update) | async-done | bytes 3145744 | tf_op jit(solution)/shard_map/all_gather | solution.py:74
  91.5 5.5 %fusion.47 = f32[256,3,512]{2,0,1:T(8,128)} fusion(bf16[256,3,2048]{2,0,1:T(8,128)(2,1)} %all-gather.5.cloned.1.call-done, bf16[2048,512]{1,0:T(8,128)(2,1)} %param.25), kind=kOutput, calls=%fused_computation.55 | convolution fusion | flops 1610612736 | bytes 6815744 | tf_op jit(solution)/shard_map/trd,dc->trc/dot_general | solution.py:77
  97.0 3.1 reshape.241
  100.1 3.7 %copy.57 = f32[256,3,2,256]{0,3,2,1:T(8,128)} copy(f32[256,3,2,256]{3,2,0,1:T(2,128)} %reshape.241) | data formatting | bytes 3145728 | tf_op jit(solution)/shard_map/reshape | solution.py:80
  103.8 2.3 multiply_reduce_fusion.2
  106.1 3.2 %multiply_reduce_fusion.3 = (f32[256,3]{0,1:T(4,128)S(1)}, f32[256,3,256]{0,2,1:T(8,128)S(1)}) fusion(bf16[256,3,2048]{2,0,1:T(8,128)(2,1)} %all-gather.5.cloned.1.call-done, bf16[2048,256]{1,0:T(8,128)(2,1)} %param.26), kind=kOutput, calls=%fused_computation.89 | convolution fusion | flops 805698816 | bytes 4983808 | tf_op jit(solution)/shard_map/trd,dc->trc/dot_general | solution.py:82
  109.9 1.0 broadcast_select_fusion
  112.7 1.6 multiply_multiply_fusion.1
  115.5 2.1 broadcast_select_fusion.1
  118.1 44.9 %while.11 = (s32[]{:T(128)}, bf16[3,256,512]{1,2,0:T(8,128)(2,1)}, s32[3]{0:T(128)}, bf16[3,1024,512]{2,1,0:T(8,128)(2,1)}, bf16[256,3,256]{0,2,1:T(8,128)(2,1)}...) while((s32[]{:T(128)}, bf16[3,256,512]{1,2,0:T(8,128)(2,1)}, ...), condition=%wide.region_6.7_spmd.clone, body=%wide.region_3.6_spmd.clone.sunk | while | flops 678690048 | bytes 27798776 | solution.py:159
  118.1 1.2 dynamic_slice.59
  121.2 1.0 constant_dynamic-slice_fusion.7
  123.0 1.3 dynamic-slice_bitcast_fusion.2
  127.3 1.5 copy-done.2
  129.9 2.4 fusion.118
  133.1 1.2 dynamic_slice.59
  136.2 1.0 constant_dynamic-slice_fusion.7
  137.9 1.3 dynamic-slice_bitcast_fusion.2
  142.3 1.5 copy-done.2
  144.9 2.4 fusion.118
  148.0 1.2 dynamic_slice.59
  152.9 1.3 dynamic-slice_bitcast_fusion.2
  157.3 1.5 copy-done.2
  159.9 2.4 fusion.118
  163.0 4.6 %fusion.43 = bf16[256,3,2048]{2,0,1:T(8,128)(2,1)} fusion(bf16[3,256,512]{1,2,0:T(8,128)(2,1)} %get-tuple-element.49, bf16[512,2048]{1,0:T(8,128)(2,1)S(1)} %copy-done), kind=kOutput, calls=%fused_computation.48 | convolution fusion | flops 1612185600 | bytes 6029312 | tf_op jit(solution)/shard_map/rtc,cd->trd/dot_general | solution.py:162
  168.7 2.2 multiply_reduce_fusion.1
  170.9 34.9 %reduce-scatter.3.cloned.1.call-done = bf16[64,3,2048]{2,0,1:T(8,128)(2,1)} async-done(((bf16[256,3,2048]{2,0,1:T(8,128)(2,1)}), bf16[64,3,2048]{2,0,1:T(8,128)(2,1)}) %reduce-scatter.3.cloned.1.call-update) | async-done | bytes 786448 | tf_op jit(solution)/shard_map/reduce_scatter | solution.py:161
  205.8 1.4 fusion.53
  207.2 2.5 multiply_reduce_fusion
  210.0 11.4 %collective-permute-done.1 = bf16[64,3,2048]{2,0,1:T(8,128)(2,1)S(1)} collective-permute-done((bf16[64,3,2048]{2,0,1:T(8,128)(2,1)S(1)}, bf16[64,3,2048]{2,0,1:T(8,128)(2,1)S(1)}, u32[]{:S(2)}, u32[]{:S(2)}) %collective-permute-start.1) | collective-permute-done | bytes 786464 | tf_op jit(solution)/shard_map/ppermute | solution.py:182
  221.4 11.5 %collective-permute-done.2 = bf16[64,3,2048]{2,0,1:T(8,128)(2,1)} collective-permute-done((bf16[64,3,2048]{2,0,1:T(8,128)(2,1)S(1)}, bf16[64,3,2048]{2,0,1:T(8,128)(2,1)}, u32[]{:S(2)}, u32[]{:S(2)}) %collective-permute-start.2) | collective-permute-done | bytes 786464 | tf_op jit(solution)/shard_map/ppermute | solution.py:182
  232.9 11.7 %collective-permute-done.3 = bf16[64,3,2048]{2,0,1:T(8,128)(2,1)} collective-permute-done((bf16[64,3,2048]{2,0,1:T(8,128)(2,1)}, bf16[64,3,2048]{2,0,1:T(8,128)(2,1)}, u32[]{:S(2)}, u32[]{:S(2)}) %collective-permute-start.3) | collective-permute-done | bytes 786464 | tf_op jit(solution)/shard_map/ppermute | solution.py:182
  244.6 1.2 constant_dynamic-update-slice_fusion.8
  245.8 1.2 constant_dynamic-update-slice_fusion.7
  247.3 1.2 constant_dynamic-update-slice_fusion.4
  248.5 1.4 constant_dynamic-update-slice_fusion.3
  250.2 2.7 copy-done.9
  252.8 5.1 %fusion.29 = f32[256,3,1024]{2,0,1:T(8,128)} fusion(bf16[2048,1024]{1,0:T(8,128)(2,1)S(1)} %copy-done.18, bf16[512,3,2048]{2,0,1:T(8,128)(2,1)S(1)} %constant_dynamic-update-slice_fusion.1, s32[]{:T(128)S(6)} %select_n.101), kind=kOutput, calls=%fused_computation.34 | convolution fusion | flops 3221225472 | bytes 10485764 | tf_op jit(solution)/shard_map/ghc,cu->ghu/dot_general | solution.py:186
  257.9 12.8 %fusion.31 = bf16[256,3,2048]{2,0,1:T(8,128)(2,1)} fusion(bf16[1024,2048]{1,0:T(8,128)(2,1)} %param.38, f32[256,3,1024]{2,0,1:T(8,128)} %fusion.29, bf16[2048,1024]{1,0:T(8,128)(2,1)} %param.37, bf16[512,3,2048]{2,0,1:T(8,128)(2,1)} %copy-done.9, s32[]{:T(128)S(6)} %select_n.101), kind=kOutput, calls=%fused_computation.37 | convolution fusion | flops 6451888128 | bytes 17825796 | tf_op jit(solution)/shard_map/wjk,kx->wjx/dot_general | solution.py:195
  272.6 36.2 %reduce-scatter.5.cloned.1.call-done = bf16[64,3,2048]{2,0,1:T(8,128)(2,1)} async-done(((bf16[256,3,2048]{2,0,1:T(8,128)(2,1)}), bf16[64,3,2048]{2,0,1:T(8,128)(2,1)}) %reduce-scatter.5.cloned.1.call-update) | async-done | bytes 786448 | tf_op jit(solution)/shard_map/reduce_scatter | solution.py:194
  308.8 1.4 fusion.55
  310.2 2.9 fusion.59
  (131 shorter events, 27.2 us)
Async XLA Ops:
  7.2 155.9 %copy-start = (bf16[512,2048]{1,0:T(8,128)(2,1)S(1)}, bf16[512,2048]{1,0:T(8,128)(2,1)}, u32[]{:S(2)}) copy-start(bf16[512,2048]{1,0:T(8,128)(2,1)} %param.29) | copy-start | bytes 6291460
  7.2 3.4 %copy-start.4 = (bf16[64,3,2048]{2,0,1:T(8,128)(2,1)S(1)}, bf16[64,3,2048]{2,0,1:T(8,128)(2,1)}, u32[]{:S(2)}) copy-start(bf16[64,3,2048]{2,0,1:T(8,128)(2,1)} %param.23) | copy-start | bytes 2359300
  7.2 5.3 %copy-start.20 = (s32[2,8]{1,0:T(2,128)S(1)}, s32[2,8]{1,0:T(2,128)}, u32[]{:S(2)}) copy-start(s32[2,8]{1,0:T(2,128)} %param.40) | copy-start | bytes 196
  7.2 5.3 %copy-start.19 = (s32[2,8]{1,0:T(2,128)S(1)}, s32[2,8]{1,0:T(2,128)}, u32[]{:S(2)}) copy-start(s32[2,8]{1,0:T(2,128)} %param.41) | copy-start | bytes 196
  7.2 5.3 %copy-start.21 = (s32[3]{0:T(128)S(1)}, s32[3]{0:T(128)}, u32[]{:S(2)}) copy-start(s32[3]{0:T(128)} %param.42) | copy-start | bytes 40
  7.2 5.7 %copy-start.22 = (s32[3]{0:T(128)S(1)}, s32[3]{0:T(128)}, u32[]{:S(2)}) copy-start(s32[3]{0:T(128)} %param.43) | copy-start | bytes 40
  7.2 55.6 %all-gather.3.cloned.1.call-start = ((), (), s32[]{:S(2)}) async-start(), calls=%async_computation.2 | async-start | bytes 2359296 | tf_op jit(solution)/shard_map/all_gather | solution.py:107
  9.2 82.3 %all-gather.5.cloned.1.call-start = ((), (), s32[]{:S(2)}) async-start(), calls=%async_computation.3 | async-start | bytes 3932160 | tf_op jit(solution)/shard_map/all_gather | solution.py:74
  12.4 193.4 %reduce-scatter.3.cloned.1.call-start = ((), (), s32[]{:S(2)}) async-start(), calls=%async_computation.4 | async-start | bytes 3932160 | tf_op jit(solution)/shard_map/reduce_scatter | solution.py:161
  106.1 3.3 %copy-start.17 = (f32[256]{0:T(256)S(1)}, f32[256]{0:T(256)}, u32[]{:S(2)}) copy-start(f32[256]{0:T(256)} %param.28) | copy-start | bytes 3076
  109.3 0.6 copy-start.16
  109.5 3.1 copy-start.15
  111.0 4.5 %collective-permute-start = (bf16[256,3,256]{0,2,1:T(8,128)(2,1)}, bf16[256,3,256]{0,2,1:T(8,128)(2,1)}, u32[]{:S(2)}, u32[]{:S(2)}) collective-permute-start(bf16[256,3,256]{0,2,1:T(8,128)(2,1)} %get-tuple-element.125), channel_id=1, source_target_pairs={{0,1},{1,0},{2,3},{3,2},{4,5},{5,4},{6,7},{7,6},{8,9},{9,8},{10,11... | collective-permute-start | bytes 1179656 | tf_op jit(solution)/shard_map/ppermute | solution.py:14
  114.5 3.6 %copy-start.23 = (s32[3]{0:T(128)S(1)}, s32[3]{0:T(128)}, u32[]{:S(2)}) copy-start(s32[3]{0:T(128)} %param.43) | copy-start | bytes 40
  122.9 3.8 %copy-start.5 = (bf16[256,1,256]{2,0,1:T(8,128)(2,1)S(1)}, bf16[256,1,256]{2,0,1:T(8,128)(2,1)}, u32[]{:S(2)}) copy-start(bf16[256,1,256]{2,0,1:T(8,128)(2,1)} %copy.76) | copy-start | bytes 393220 | tf_op jit(solution)/shard_map/while
  127.3 1.5 copy-start.2
  137.9 3.8 %copy-start.5 = (bf16[256,1,256]{2,0,1:T(8,128)(2,1)S(1)}, bf16[256,1,256]{2,0,1:T(8,128)(2,1)}, u32[]{:S(2)}) copy-start(bf16[256,1,256]{2,0,1:T(8,128)(2,1)} %copy.76) | copy-start | bytes 393220 | tf_op jit(solution)/shard_map/while
  142.3 1.5 copy-start.2
  152.9 3.8 %copy-start.5 = (bf16[256,1,256]{2,0,1:T(8,128)(2,1)S(1)}, bf16[256,1,256]{2,0,1:T(8,128)(2,1)}, u32[]{:S(2)}) copy-start(bf16[256,1,256]{2,0,1:T(8,128)(2,1)} %copy.76) | copy-start | bytes 393220 | tf_op jit(solution)/shard_map/while
  157.3 1.5 copy-start.2
  167.6 0.9 copy-start.7
  167.6 1.0 copy-start.8
  167.6 1.0 copy-start.10
  167.7 39.5 %copy-start.12 = (f32[2048]{0:T(1024)S(1)}, f32[2048]{0:T(1024)}, u32[]{:S(2)}) copy-start(f32[2048]{0:T(1024)} %param.33) | copy-start | bytes 24580
  167.7 39.5 %copy-start.13 = (f32[2048]{0:T(1024)S(1)}, f32[2048]{0:T(1024)}, u32[]{:S(2)}) copy-start(f32[2048]{0:T(1024)} %param.30) | copy-start | bytes 24580
  167.7 141.1 %reduce-scatter.5.cloned.1.call-start = ((), (), s32[]{:S(2)}) async-start(), calls=%async_computation.5 | async-start | bytes 3932160 | tf_op jit(solution)/shard_map/reduce_scatter | solution.py:194
  207.2 2.5 copy-start.11
  209.7 40.3 %copy-start.3 = (f32[64,3,2048]{2,0,1:T(8,128)}, f32[64,3,2048]{2,0,1:T(8,128)S(1)}, u32[]{:S(2)}) copy-start(f32[64,3,2048]{2,0,1:T(8,128)S(1)} %get-tuple-element.127) | copy-start | bytes 4718596
  209.9 11.5 %collective-permute-start.1 = (bf16[64,3,2048]{2,0,1:T(8,128)(2,1)S(1)}, bf16[64,3,2048]{2,0,1:T(8,128)(2,1)S(1)}, u32[]{:S(2)}, u32[]{:S(2)}) collective-permute-start(bf16[64,3,2048]{2,0,1:T(8,128)(2,1)S(1)} %multiply_convert_fusion), channel_id=1, source_target_pairs={{0,1},{1,2},{2,3},{3,0},{4,5},{5,6},{6,7},{7,4},{8,9},{9,10},{10,1... | collective-permute-start | bytes 2359304 | tf_op jit(solution)/shard_map/ppermute | solution.py:182
  221.4 11.5 %collective-permute-start.2 = (bf16[64,3,2048]{2,0,1:T(8,128)(2,1)S(1)}, bf16[64,3,2048]{2,0,1:T(8,128)(2,1)}, u32[]{:S(2)}, u32[]{:S(2)}) collective-permute-start(bf16[64,3,2048]{2,0,1:T(8,128)(2,1)S(1)} %collective-permute-done.1), channel_id=1, source_target_pairs={{0,1},{1,2},{2,3},{3,0},{4,5},{5,6},{6,7},{7,4},{8,9},{9,10},{10,1... | collective-permute-start | bytes 2359304 | tf_op jit(solution)/shard_map/ppermute | solution.py:182
  232.9 11.7 %collective-permute-start.3 = (bf16[64,3,2048]{2,0,1:T(8,128)(2,1)}, bf16[64,3,2048]{2,0,1:T(8,128)(2,1)}, u32[]{:S(2)}, u32[]{:S(2)}) collective-permute-start(bf16[64,3,2048]{2,0,1:T(8,128)(2,1)} %collective-permute-done.2), channel_id=1, source_target_pairs={{0,1},{1,2},{2,3},{3,0},{4,5},{5,6},{6,7},{7,4},{8,9},{9,10},{10,1... | collective-permute-start | bytes 2359304 | tf_op jit(solution)/shard_map/ppermute | solution.py:182
  248.5 4.3 %copy-start.18 = (bf16[2048,1024]{1,0:T(8,128)(2,1)S(1)}, bf16[2048,1024]{1,0:T(8,128)(2,1)}, u32[]{:S(2)}) copy-start(bf16[2048,1024]{1,0:T(8,128)(2,1)} %param.36) | copy-start | bytes 12582916
  250.2 2.7 copy-start.9
  270.7 1.0 copy-start.6
  270.7 39.5 %copy-start.14 = (f32[2048]{0:T(1024)S(1)}, f32[2048]{0:T(1024)}, u32[]{:S(2)}) copy-start(f32[2048]{0:T(1024)} %param.35) | copy-start | bytes 24580
  271.7 41.5 %copy-start.1 = (bf16[512,2048]{1,0:T(8,128)(2,1)S(1)}, bf16[512,2048]{1,0:T(8,128)(2,1)}, u32[]{:S(2)}) copy-start(bf16[512,2048]{1,0:T(8,128)(2,1)} %param.29) | copy-start | bytes 6291460
Sparse Core Ops, SparseCore 0:
  10.8 52.0 all-gather.2
  64.4 27.0 all-gather.4
  167.8 37.9 reduce-scatter.2
  270.8 37.9 reduce-scatter.4
